TPU v7x, 32 devices: a whole 2x2x4 slice. The times are simulated.
32 devices in a mesh: groups: 2 (over y), gx: 4 (over z), gy: 2 (over x), gz: 2 (over core).
Axes of the slice: x: 2, y: 2, z: 4, core: 2. Of those that a mesh axis runs over, the one named last changes fastest.
Arguments:
- earlier_warmth_field: float32 [16, 512, 512], P(('groups', 'gz'), 'gy', 'gx'), parts along dimension 0, may hold values from -6 to 6
- caloric_storage: float32 [16, 512, 512], P(('groups', 'gz'), 'gy', 'gx'), parts along dimension 0, may hold values from 0.5 to 4
- thermal_diffusivity_coefficient: float32 [16, 512, 512], P(('groups', 'gz'), 'gy', 'gx'), parts along dimension 0, may hold values from 0.3 to 3
- dissipation_catalog: float32 [16, 64, 128], P('groups'), parts along dimension 0, may hold values from 0.1 to 3
- dissipation_selector: int32 [16, 8, 4], P(('groups', 'gz'), 'gy', 'gx'), parts along dimension 0, may hold values from 0 to 7
- refine_depth: int32 [16, 8, 4], P(('groups', 'gz'), 'gy', 'gx'), parts along dimension 0, may hold values from 1 to 4, as said below
- border_band_width: int32 [16, 4], P(('groups', 'gy'), 'gx'), parts along dimension 0, may hold values from 1 to 16
- microflow_flag: int32 [16], P(('groups', 'gz')), parts along dimension 0, may hold values 0 or 1
Outputs:
- warmth_solution: float32 [16, 512, 512], P(('groups', 'gz'), 'gy', 'gx'), parts along dimension 0
- leftover_misfit: float32 [16, 512, 512], P(('groups', 'gz'), 'gy', 'gx'), parts along dimension 0
There are 2 independent parts, one for each index of `groups`. A program takes and returns all parts, laid end to end along the dimension named above; each array names one. Nothing has to cross between parts.
Inputs may be any that keep to these rules, and one draw needn't show every extreme that they name: `refine_depth`: each tile's level is 1, 2 or 4.
All inputs are finite; a program needn't handle non-finite values. No bound on the sum of `microflow_flag` on one device may be relied on, other than what follows from the above.
Results may differ from a plain program's by a relative error of at most 0.00022.
Values sent between devices are 32-bit elements; how exact they have to be, the bound alone decides.
No kernel may reach another device: no remote copies, remote signals or barrier semaphores. Data moves between devices by JAX's collectives and lax.ppermute only.
A program may use at most 64 MiB of HBM per device.

v0:
```python
import jax
import jax.numpy as jnp
from jax import lax
from jax.sharding import PartitionSpec as P

TY = 64
ITERS = 2
interval_increment = 0.5
vertical_ratio = 2.0
coolant_film = 1.5
band_sink = 1.0
damping = 0.8


def with_halo(shard, sides, width):
    for axis, dim in sides:
        count, length = (lax.axis_size(axis), shard.shape[dim])
        up = [(i, (i + 1) % count) for i in range(count - 1)]
        down = [(j, i) for i, j in up]
        last = lax.slice_in_dim(shard, length - width, length, axis=dim)
        first = lax.slice_in_dim(shard, 0, width, axis=dim)
        before = lax.ppermute(last, axis, up)
        after = lax.ppermute(first, axis, down)
        shard = jnp.concatenate([before, shard, after], axis=dim)
    return shard


def harmonic(first, second):
    return 2.0 * first * second / (first + second)


def neighbours(padded):
    return (
        padded[:-2, 1:-1, 1:-1],
        padded[2:, 1:-1, 1:-1],
        padded[1:-1, :-2, 1:-1],
        padded[1:-1, 2:, 1:-1],
        padded[1:-1, 1:-1, :-2],
        padded[1:-1, 1:-1, 2:],
    )


def body(
    earlier_warmth_field,
    caloric_storage,
    thermal_diffusivity_coefficient,
    dissipation_catalog,
    dissipation_selector,
    refine_depth,
    border_band_width,
    microflow_flag,
):
    stacked_layers, vertical_count, horizontal_count = earlier_warmth_field.shape
    kappa_rim = with_halo(thermal_diffusivity_coefficient, (("gx", 2), ("gy", 1), ("gz", 0)), 1)
    faces = [harmonic(thermal_diffusivity_coefficient, other) for other in neighbours(kappa_rim)]
    faces[0] = vertical_ratio * faces[0]
    faces[1] = vertical_ratio * faces[1]
    edge_cells = jnp.repeat(border_band_width, TY, axis=0)
    row_tile = (jnp.arange(vertical_count, dtype=jnp.int32) % TY)[:, None]
    band = ((row_tile < edge_cells) | (row_tile >= TY - edge_cells)).astype(jnp.float32)
    sink = coolant_film * microflow_flag.astype(jnp.float32)[:, None, None] + band_sink * band[None]
    diagonal = caloric_storage / interval_increment + sink
    for face in faces:
        diagonal = diagonal + face
    column_patch = jnp.arange(horizontal_count, dtype=jnp.int32)
    tile_faces = (
        faces[2] * (row_tile != 0).astype(jnp.float32),
        faces[3] * (row_tile != TY - 1).astype(jnp.float32),
        faces[4] * (column_patch != 0).astype(jnp.float32),
        faces[5] * (column_patch != horizontal_count - 1).astype(jnp.float32),
    )
    level_cells = jnp.repeat(refine_depth, TY, axis=1)
    map_count = dissipation_catalog.shape[0]
    onehot = (dissipation_selector[:, :, 0, None] == jnp.arange(map_count, dtype=jnp.int32)).astype(
        jnp.float32
    )
    dissipation_density = jnp.einsum(
        "zjp,pyx->zjyx", onehot, dissipation_catalog, precision=lax.Precision.HIGHEST
    ).reshape(stacked_layers, vertical_count, horizontal_count)
    linear_source_term = (
        caloric_storage / interval_increment * earlier_warmth_field + dissipation_density
    )

    def linear_map_action(field):
        padded = with_halo(field, (("gx", 2), ("gy", 1), ("gz", 0)), 1)
        total = diagonal * field
        for face, other in zip(faces, neighbours(padded)):
            total = total - face * other
        return total

    def smooth(vector):
        state = damping * vector / diagonal
        for sweep in range(1, 4):
            padded = jnp.pad(state, ((0, 0), (1, 1), (1, 1)))
            inner = tile_faces[0] * padded[:, :-2, 1:-1] + tile_faces[1] * padded[:, 2:, 1:-1]
            inner = (
                inner + tile_faces[2] * padded[:, 1:-1, :-2] + tile_faces[3] * padded[:, 1:-1, 2:]
            )
            fresh = (1.0 - damping) * state + damping * (vector + inner) / diagonal
            state = jnp.where(level_cells > sweep, fresh, state)
        return state

    warmth_solution = earlier_warmth_field
    leftover_misfit = linear_source_term - linear_map_action(warmth_solution)
    smoothed = smooth(leftover_misfit)
    applied = linear_map_action(smoothed)
    for turn in range(ITERS):
        gamma_now, delta_now = lax.psum(
            (jnp.sum(leftover_misfit * smoothed), jnp.sum(applied * smoothed)), ("gx", "gy", "gz")
        )
        pre = smooth(applied)
        twice = linear_map_action(pre)
        if turn == 0:
            present_stride_amount = gamma_now / delta_now
            image_dir, smooth_dir, operator_times_direction, conjugate_update_heading = (
                twice,
                pre,
                applied,
                smoothed,
            )
        else:
            current_mixing_factor = gamma_now / gamma_prev
            present_stride_amount = gamma_now / (
                delta_now - current_mixing_factor * gamma_now / alpha_prev
            )
            image_dir = twice + current_mixing_factor * image_dir
            smooth_dir = pre + current_mixing_factor * smooth_dir
            operator_times_direction = applied + current_mixing_factor * operator_times_direction
            conjugate_update_heading = smoothed + current_mixing_factor * conjugate_update_heading
        warmth_solution = warmth_solution + present_stride_amount * conjugate_update_heading
        leftover_misfit = leftover_misfit - present_stride_amount * operator_times_direction
        if turn + 1 < ITERS:
            smoothed = smoothed - present_stride_amount * smooth_dir
            applied = linear_map_action(smoothed)
        gamma_prev, alpha_prev = (gamma_now, present_stride_amount)
    return (warmth_solution, leftover_misfit)


def solution(mesh):
    return jax.shard_map(
        body,
        mesh=mesh,
        in_specs=(
            P(("groups", "gz"), "gy", "gx"),
            P(("groups", "gz"), "gy", "gx"),
            P(("groups", "gz"), "gy", "gx"),
            P("groups", None, None),
            P(("groups", "gz"), "gy", "gx"),
            P(("groups", "gz"), "gy", "gx"),
            P(("groups", "gy"), "gx"),
            P(("groups", "gz")),
        ),
        out_specs=(P(("groups", "gz"), "gy", "gx"), P(("groups", "gz"), "gy", "gx")),
        check_vma=False,
    )
```

profile of v0, /device:TPU:0, one launch (start us, length us, event | category | flops | bytes accessed | tf_op | source)
XLA Modules:
  0.0 202.6 jit_solution(9930890958993695138)
XLA Ops:
  0.6 2.4 %fusion.120 = (f32[4,256,1]{2,1,0:T(8,128)}, f32[4,256,1]{2,1,0:T(8,128)}) fusion(f32[4,256,128]{2,1,0:T(8,128)} %param.10), kind=kLoop, calls=%fused_computation.277 | loop fusion | bytes 16384 | tf_op jit(solution)/shard_map/slice | solution.py:20
  3.0 5.0 %collective-permute-start = (f32[4,256,1]{2,1,0:T(8,128)}, f32[4,256,1]{2,1,0:T(8,128)S(1)}, u32[]{:S(2)}, u32[]{:S(2)}) collective-permute-start(f32[4,256,1]{2,1,0:T(8,128)} %get-tuple-element.41), channel_id=1, source_target_pairs={{0,4},{4,8},{8,12},{1,5},{5,9},{9,13},{2,6},{6,10},{10,14},{3,7},{... | collective-permute-start | bytes 12296 | tf_op jit(solution)/shard_map/ppermute | solution.py:22
  8.1 1.4 collective-permute-start.1
  9.5 1.1 fusion.121
  10.6 4.7 %collective-permute-start.6 = (f32[4,256,1]{2,1,0:T(8,128)}, f32[4,256,1]{2,1,0:T(8,128)S(1)}, u32[]{:S(2)}, u32[]{:S(2)}) collective-permute-start(f32[4,256,1]{2,1,0:T(8,128)} %get-tuple-element.43), channel_id=1, source_target_pairs={{0,4},{4,8},{8,12},{1,5},{5,9},{9,13},{2,6},{6,10},{10,14},{3,7},{... | collective-permute-start | bytes 12296 | tf_op jit(solution)/shard_map/ppermute | solution.py:22
  15.3 1.3 collective-permute-start.7
  17.5 3.1 %collective-permute-done = f32[4,256,1]{2,1,0:T(8,128)S(1)} collective-permute-done((f32[4,256,1]{2,1,0:T(8,128)}, f32[4,256,1]{2,1,0:T(8,128)S(1)}, u32[]{:S(2)}, u32[]{:S(2)}) %collective-permute-start) | collective-permute-done | bytes 4128 | tf_op jit(solution)/shard_map/ppermute | solution.py:22
  20.6 4.5 %collective-permute-done.1 = f32[4,256,1]{2,1,0:T(8,128)S(1)} collective-permute-done((f32[4,256,1]{2,1,0:T(8,128)}, f32[4,256,1]{2,1,0:T(8,128)S(1)}, u32[]{:S(2)}, u32[]{:S(2)}) %collective-permute-start.1) | collective-permute-done | bytes 4128 | tf_op jit(solution)/shard_map/ppermute | solution.py:23
  25.2 3.4 %collective-permute-start.2 = (f32[4,1,130]{2,1,0:T(1,128)S(1)}, f32[4,1,130]{2,1,0:T(1,128)S(1)}, u32[]{:S(2)}, u32[]{:S(2)}) collective-permute-start(f32[4,1,130]{2,1,0:T(1,128)S(1)} %get-tuple-element.33), channel_id=1, source_target_pairs={{0,2},{1,3},{4,6},{5,7},{8,10},{9,11},{12,14},{13,15},{16,18},{17,... | collective-permute-start | bytes 6248 | tf_op jit(solution)/shard_map/ppermute | solution.py:22
  28.6 1.3 collective-permute-start.3
  30.7 4.2 %collective-permute-done.7 = f32[4,256,1]{2,1,0:T(8,128)S(1)} collective-permute-done((f32[4,256,1]{2,1,0:T(8,128)}, f32[4,256,1]{2,1,0:T(8,128)S(1)}, u32[]{:S(2)}, u32[]{:S(2)}) %collective-permute-start.7) | collective-permute-done | bytes 4128 | tf_op jit(solution)/shard_map/ppermute | solution.py:23
  35.0 3.4 %collective-permute-start.8 = (f32[4,1,130]{2,1,0:T(1,128)S(1)}, f32[4,1,130]{2,1,0:T(1,128)S(1)}, u32[]{:S(2)}, u32[]{:S(2)}) collective-permute-start(f32[4,1,130]{2,1,0:T(1,128)S(1)} %get-tuple-element.35), channel_id=1, source_target_pairs={{0,2},{1,3},{4,6},{5,7},{8,10},{9,11},{12,14},{13,15},{16,18},{17,... | collective-permute-start | bytes 6248 | tf_op jit(solution)/shard_map/ppermute | solution.py:22
  38.4 1.3 collective-permute-start.9
  39.8 1.1 pad_maximum_fusion.87
  40.9 1.3 collective-permute-start.4
  42.2 1.3 collective-permute-start.5
  44.2 2.6 %collective-permute-start.10 = (f32[1,258,130]{2,1,0:T(8,128)S(1)}, f32[1,258,130]{2,1,0:T(8,128)S(1)}, u32[]{:S(2)}, u32[]{:S(2)}) collective-permute-start(f32[1,258,130]{2,1,0:T(8,128)S(1)} %get-tuple-element.27), channel_id=1, source_target_pairs={{0,1},{2,3},{4,5},{6,7},{8,9},{10,11},{12,13},{14,15},{16,17},{18,... | collective-permute-start | bytes 402488 | tf_op jit(solution)/shard_map/ppermute | solution.py:22
  46.9 1.3 collective-permute-start.11
  48.2 0.9 copy.12
  51.0 7.1 %multiply_divide_fusion.1 = (f32[4,256,128]{2,1,0:T(8,128)S(1)}, f32[4,256,128]{2,1,0:T(8,128)S(1)}, f32[4,256,128]{2,1,0:T(8,128)S(1)}, f32[4,256,128]{2,1,0:T(...) fusion(f32[4,256,1]{2,1,0:T(8,128)} %copy-done.16, ...), kind=kLoop, calls=%fused_computation.215 | loop fusion | flops 10878976 | bytes 7381184 | tf_op jit(solution)/shard_map/div | solution.py:92
  60.0 3.5 %collective-permute-start.12 = (f32[4,256,1]{2,1,0:T(8,128)S(1)}, f32[4,256,1]{2,1,0:T(8,128)S(1)}, u32[]{:S(2)}, u32[]{:S(2)}) collective-permute-start(f32[4,256,1]{2,1,0:T(8,128)S(1)} %get-tuple-element.39), channel_id=1, source_target_pairs={{0,4},{4,8},{8,12},{1,5},{5,9},{9,13},{2,6},{6,10},{10,14},{3,7},{... | collective-permute-start | bytes 12296 | tf_op jit(solution)/shard_map/ppermute | solution.py:22
  63.5 1.3 collective-permute-start.13
  64.8 10.1 %collective-permute-done.12 = f32[4,256,1]{2,1,0:T(8,128)S(1)} collective-permute-done((f32[4,256,1]{2,1,0:T(8,128)S(1)}, f32[4,256,1]{2,1,0:T(8,128)S(1)}, u32[]{:S(2)}, u32[]{:S(2)}) %collective-permute-start.12) | collective-permute-done | bytes 4128 | tf_op jit(solution)/shard_map/ppermute | solution.py:22
  74.9 4.7 %collective-permute-done.13 = f32[4,256,1]{2,1,0:T(8,128)S(1)} collective-permute-done((f32[4,256,1]{2,1,0:T(8,128)S(1)}, f32[4,256,1]{2,1,0:T(8,128)S(1)}, u32[]{:S(2)}, u32[]{:S(2)}) %collective-permute-start.13) | collective-permute-done | bytes 4128 | tf_op jit(solution)/shard_map/ppermute | solution.py:23
  79.7 4.5 %collective-permute-start.14 = (f32[4,1,130]{2,1,0:T(1,128)S(1)}, f32[4,1,130]{2,1,0:T(1,128)S(1)}, u32[]{:S(2)}, u32[]{:S(2)}) collective-permute-start(f32[4,1,130]{2,1,0:T(1,128)S(1)} %get-tuple-element.31), channel_id=1, source_target_pairs={{0,2},{1,3},{4,6},{5,7},{8,10},{9,11},{12,14},{13,15},{16,18},{17,... | collective-permute-start | bytes 6248 | tf_op jit(solution)/shard_map/ppermute | solution.py:22
  84.3 1.3 collective-permute-start.15
  85.6 4.2 %collective-permute-done.15 = f32[4,1,130]{2,1,0:T(1,128)S(1)} collective-permute-done((f32[4,1,130]{2,1,0:T(1,128)S(1)}, f32[4,1,130]{2,1,0:T(1,128)S(1)}, u32[]{:S(2)}, u32[]{:S(2)}) %collective-permute-start.15) | collective-permute-done | bytes 2112 | tf_op jit(solution)/shard_map/ppermute | solution.py:23
  90.1 1.3 collective-permute-start.16
  91.4 1.3 collective-permute-start.17
  92.7 2.1 %collective-permute-done.17 = f32[1,258,130]{2,1,0:T(8,128)S(1)} collective-permute-done((f32[1,258,130]{2,1,0:T(8,128)S(1)}, f32[1,258,130]{2,1,0:T(8,128)S(1)}, u32[]{:S(2)}, u32[]{:S(2)}) %collective-permute-start.17) | collective-permute-done | bytes 134192 | tf_op jit(solution)/shard_map/ppermute | solution.py:23
  94.8 1.7 multiply_reduce_fusion.2
  97.4 1.4 fusion.56
  98.7 30.3 %all-reduce.7 = (f32[]{:T(128)}, f32[]{:T(128)}) all-reduce(f32[]{:T(128)} %get-tuple-element.5, f32[]{:T(128)} %get-tuple-element.4), channel_id=1, replica_groups=mesh['groups'=2,'gx'=4,'gy'=2,'gz'=2] {'gx','gy','gz'}, use_global_device_ids=true, to_apply=%region_1.2 | all-reduce | flops 2 | bytes 16 | tf_op jit(solution)/shard_map/psum | solution.py:108
  130.3 2.9 %multiply_subtract_fusion.1 = f32[4,256,128]{2,1,0:T(8,128)S(1)} fusion(f32[4,256,128]{2,1,0:T(8,128)S(1)} %fusion.32, f32[4,256,128]{2,1,0:T(8,128)} %fusion.56, f32[4,256,128]{2,1,0:T(8,128)S(1)} %get-tuple-element.14, f32[4,256,128]{2,1,0:T(8,128)} %copy-done.3, f32[4,256,128]{2,1,0:T(8,128)S(1)} %get-tuple-element.20, ...), kind=kLoop, calls=%fused_computation.210 | loop fusion | flops 2490368 | bytes 4722692 | tf_op jit(solution)/shard_map/sub | solution.py:133
  133.4 1.3 collective-permute-start.18
  134.7 1.3 collective-permute-start.19
  136.0 10.0 %collective-permute-done.18 = f32[4,256,1]{2,1,0:T(8,128)S(1)} collective-permute-done((f32[4,256,1]{2,1,0:T(8,128)S(1)}, f32[4,256,1]{2,1,0:T(8,128)S(1)}, u32[]{:S(2)}, u32[]{:S(2)}) %collective-permute-start.18) | collective-permute-done | bytes 4128 | tf_op jit(solution)/shard_map/ppermute | solution.py:22
  146.0 4.1 %collective-permute-done.19 = f32[4,256,1]{2,1,0:T(8,128)S(1)} collective-permute-done((f32[4,256,1]{2,1,0:T(8,128)S(1)}, f32[4,256,1]{2,1,0:T(8,128)S(1)}, u32[]{:S(2)}, u32[]{:S(2)}) %collective-permute-start.19) | collective-permute-done | bytes 4128 | tf_op jit(solution)/shard_map/ppermute | solution.py:23
  150.3 1.3 collective-permute-start.20
  151.6 1.4 collective-permute-start.21
  153.0 4.2 %collective-permute-done.21 = f32[4,1,130]{2,1,0:T(1,128)S(1)} collective-permute-done((f32[4,1,130]{2,1,0:T(1,128)S(1)}, f32[4,1,130]{2,1,0:T(1,128)S(1)}, u32[]{:S(2)}, u32[]{:S(2)}) %collective-permute-start.21) | collective-permute-done | bytes 2112 | tf_op jit(solution)/shard_map/ppermute | solution.py:23
  157.5 1.3 collective-permute-start.22
  158.8 1.3 collective-permute-start.23
  160.1 2.1 %collective-permute-done.23 = f32[1,258,130]{2,1,0:T(8,128)S(1)} collective-permute-done((f32[1,258,130]{2,1,0:T(8,128)S(1)}, f32[1,258,130]{2,1,0:T(8,128)S(1)}, u32[]{:S(2)}, u32[]{:S(2)}) %collective-permute-start.23) | collective-permute-done | bytes 134192 | tf_op jit(solution)/shard_map/ppermute | solution.py:23
  162.3 2.5 %multiply_reduce_fusion = (f32[]{:T(128)}, f32[]{:T(128)}, f32[4,256,128]{2,1,0:T(8,128)}) fusion(f32[4,256,128]{2,1,0:T(8,128)S(1)} %multiply_subtract_fusion.1, f32[4,256,128]{2,1,0:T(8,128)S(1)} %copy-done.1, f32[4,256,128]{2,1,0:T(8,128)S(1)} %copy-done.4, f32[]{:T(128)S(6)} %div.69, f32[4,256,128]{2,1,0:T(8,128)S(1)} %get-tuple-element.20, ...), kind=kLoop, calls=%fused_computation.208 | loop fusion | flops 4849662 | bytes 6047852 | tf_op jit(solution)/shard_map/reduce_sum | solution.py:109
  164.8 30.2 %all-reduce.6 = (f32[]{:T(128)}, f32[]{:T(128)}) all-reduce(f32[]{:T(128)} %get-tuple-element.3, f32[]{:T(128)} %get-tuple-element.2), channel_id=1, replica_groups=mesh['groups'=2,'gx'=4,'gy'=2,'gz'=2] {'gx','gy','gz'}, use_global_device_ids=true, to_apply=%region_5.6 | all-reduce | flops 2 | bytes 16 | tf_op jit(solution)/shard_map/psum | solution.py:108
  199.4 2.2 %multiply_add_fusion = f32[4,256,128]{2,1,0:T(8,128)} fusion(f32[4,256,128]{2,1,0:T(8,128)} %copy-done.6, f32[4,256,128]{2,1,0:T(8,128)S(1)} %fusion.32, f32[4,256,128]{2,1,0:T(8,128)} %param.8, f32[]{:T(128)S(6)} %div.74, f32[]{:T(128)S(6)} %div.76, f32[]{:T(128)S(6)} %div.69), kind=kLoop, calls=%fused_computation.207 | loop fusion | flops 786432 | bytes 2097164 | tf_op jit(solution)/shard_map/add | solution.py:130
  201.7 0.9 multiply_subtract_fusion
  (94 shorter events, 8.2 us)
Async XLA Ops:
  0.6 8.9 %copy-start.7 = (f32[4,256,128]{2,1,0:T(8,128)S(1)}, f32[4,256,128]{2,1,0:T(8,128)}, u32[]{:S(2)}) copy-start(f32[4,256,128]{2,1,0:T(8,128)} %param.8) | copy-start | bytes 1572868
  3.0 17.6 %collective-permute-start = (f32[4,256,1]{2,1,0:T(8,128)}, f32[4,256,1]{2,1,0:T(8,128)S(1)}, u32[]{:S(2)}, u32[]{:S(2)}) collective-permute-start(f32[4,256,1]{2,1,0:T(8,128)} %get-tuple-element.41), channel_id=1, source_target_pairs={{0,4},{4,8},{8,12},{1,5},{5,9},{9,13},{2,6},{6,10},{10,14},{3,7},{... | collective-permute-start | bytes 12296 | tf_op jit(solution)/shard_map/ppermute | solution.py:22
  8.0 8.6 %copy-start.23 = (s32[4,1]{0,1:T(1,128)S(1)}, s32[4,1]{0,1:T(1,128)}, u32[]{:S(2)}) copy-start(s32[4,1]{0,1:T(1,128)} %param.14) | copy-start | bytes 52
  8.0 8.8 %copy-start.24 = (s32[4]{0:T(128)S(1)}, s32[4]{0:T(128)}, u32[]{:S(2)}) copy-start(s32[4]{0:T(128)} %param.15) | copy-start | bytes 52
  8.0 8.8 %copy-start.22 = (s32[4,4,1]{1,2,0:T(1,128)S(1)}, s32[4,4,1]{1,2,0:T(1,128)}, u32[]{:S(2)}) copy-start(s32[4,4,1]{1,2,0:T(1,128)} %param.13) | copy-start | bytes 196
  8.1 8.8 %copy-start.20 = (f32[8,64,128]{2,1,0:T(8,128)S(1)}, f32[8,64,128]{2,1,0:T(8,128)}, u32[]{:S(2)}) copy-start(f32[8,64,128]{2,1,0:T(8,128)} %param.11) | copy-start | bytes 786436
  8.1 8.8 %copy-start.21 = (s32[4,4,1]{1,2,0:T(1,128)S(1)}, s32[4,4,1]{1,2,0:T(1,128)}, u32[]{:S(2)}) copy-start(s32[4,4,1]{1,2,0:T(1,128)} %param.12) | copy-start | bytes 196
  8.1 17.0 %collective-permute-start.1 = (f32[4,256,1]{2,1,0:T(8,128)}, f32[4,256,1]{2,1,0:T(8,128)S(1)}, u32[]{:S(2)}, u32[]{:S(2)}) collective-permute-start(f32[4,256,1]{2,1,0:T(8,128)} %get-tuple-element.42), channel_id=1, source_target_pairs={{4,0},{8,4},{12,8},{5,1},{9,5},{13,9},{6,2},{10,6},{14,10},{7,3},{... | collective-permute-start | bytes 12296 | tf_op jit(solution)/shard_map/ppermute | solution.py:23
  10.6 14.5 %copy-start.8 = (f32[4,256,128]{2,1,0:T(8,128)S(1)}, f32[4,256,128]{2,1,0:T(8,128)}, u32[]{:S(2)}) copy-start(f32[4,256,128]{2,1,0:T(8,128)} %param.10) | copy-start | bytes 1572868
  10.6 20.1 %collective-permute-start.6 = (f32[4,256,1]{2,1,0:T(8,128)}, f32[4,256,1]{2,1,0:T(8,128)S(1)}, u32[]{:S(2)}, u32[]{:S(2)}) collective-permute-start(f32[4,256,1]{2,1,0:T(8,128)} %get-tuple-element.43), channel_id=1, source_target_pairs={{0,4},{4,8},{8,12},{1,5},{5,9},{9,13},{2,6},{6,10},{10,14},{3,7},{... | collective-permute-start | bytes 12296 | tf_op jit(solution)/shard_map/ppermute | solution.py:22
  15.3 19.6 %collective-permute-start.7 = (f32[4,256,1]{2,1,0:T(8,128)}, f32[4,256,1]{2,1,0:T(8,128)S(1)}, u32[]{:S(2)}, u32[]{:S(2)}) collective-permute-start(f32[4,256,1]{2,1,0:T(8,128)} %get-tuple-element.44), channel_id=1, source_target_pairs={{4,0},{8,4},{12,8},{5,1},{9,5},{13,9},{6,2},{10,6},{14,10},{7,3},{... | collective-permute-start | bytes 12296 | tf_op jit(solution)/shard_map/ppermute | solution.py:23
  20.6 19.2 %copy-start.13 = (f32[4,256,1]{2,1,0:T(8,128)}, f32[4,256,1]{2,1,0:T(8,128)S(1)}, u32[]{:S(2)}) copy-start(f32[4,256,1]{2,1,0:T(8,128)S(1)} %collective-permute-done) | copy-start | bytes 12292
  25.1 14.7 %copy-start.14 = (f32[4,256,1]{2,1,0:T(8,128)}, f32[4,256,1]{2,1,0:T(8,128)S(1)}, u32[]{:S(2)}) copy-start(f32[4,256,1]{2,1,0:T(8,128)S(1)} %collective-permute-done.1) | copy-start | bytes 12292
  25.2 14.5 %collective-permute-start.2 = (f32[4,1,130]{2,1,0:T(1,128)S(1)}, f32[4,1,130]{2,1,0:T(1,128)S(1)}, u32[]{:S(2)}, u32[]{:S(2)}) collective-permute-start(f32[4,1,130]{2,1,0:T(1,128)S(1)} %get-tuple-element.33), channel_id=1, source_target_pairs={{0,2},{1,3},{4,6},{5,7},{8,10},{9,11},{12,14},{13,15},{16,18},{17,... | collective-permute-start | bytes 6248 | tf_op jit(solution)/shard_map/ppermute | solution.py:22
  28.6 11.1 %collective-permute-start.3 = (f32[4,1,130]{2,1,0:T(1,128)S(1)}, f32[4,1,130]{2,1,0:T(1,128)S(1)}, u32[]{:S(2)}, u32[]{:S(2)}) collective-permute-start(f32[4,1,130]{2,1,0:T(1,128)S(1)} %get-tuple-element.34), channel_id=1, source_target_pairs={{2,0},{3,1},{6,4},{7,5},{10,8},{11,9},{14,12},{15,13},{18,16},{19,... | collective-permute-start | bytes 6248 | tf_op jit(solution)/shard_map/ppermute | solution.py:23
  30.7 13.2 %copy-start.15 = (f32[4,256,1]{2,1,0:T(8,128)}, f32[4,256,1]{2,1,0:T(8,128)S(1)}, u32[]{:S(2)}) copy-start(f32[4,256,1]{2,1,0:T(8,128)S(1)} %collective-permute-done.6) | copy-start | bytes 12292
  34.9 9.0 %copy-start.16 = (f32[4,256,1]{2,1,0:T(8,128)}, f32[4,256,1]{2,1,0:T(8,128)S(1)}, u32[]{:S(2)}) copy-start(f32[4,256,1]{2,1,0:T(8,128)S(1)} %collective-permute-done.7) | copy-start | bytes 12292
  35.0 8.4 %collective-permute-start.8 = (f32[4,1,130]{2,1,0:T(1,128)S(1)}, f32[4,1,130]{2,1,0:T(1,128)S(1)}, u32[]{:S(2)}, u32[]{:S(2)}) collective-permute-start(f32[4,1,130]{2,1,0:T(1,128)S(1)} %get-tuple-element.35), channel_id=1, source_target_pairs={{0,2},{1,3},{4,6},{5,7},{8,10},{9,11},{12,14},{13,15},{16,18},{17,... | collective-permute-start | bytes 6248 | tf_op jit(solution)/shard_map/ppermute | solution.py:22
  38.4 5.5 %collective-permute-start.9 = (f32[4,1,130]{2,1,0:T(1,128)S(1)}, f32[4,1,130]{2,1,0:T(1,128)S(1)}, u32[]{:S(2)}, u32[]{:S(2)}) collective-permute-start(f32[4,1,130]{2,1,0:T(1,128)S(1)} %get-tuple-element.36), channel_id=1, source_target_pairs={{2,0},{3,1},{6,4},{7,5},{10,8},{11,9},{14,12},{15,13},{18,16},{19,... | collective-permute-start | bytes 6248 | tf_op jit(solution)/shard_map/ppermute | solution.py:23
  40.9 8.7 %collective-permute-start.4 = (f32[1,258,130]{2,1,0:T(8,128)}, f32[1,258,130]{2,1,0:T(8,128)S(1)}, u32[]{:S(2)}, u32[]{:S(2)}) collective-permute-start(f32[1,258,130]{2,1,0:T(8,128)} %get-tuple-element.26), channel_id=1, source_target_pairs={{0,1},{2,3},{4,5},{6,7},{8,9},{10,11},{12,13},{14,15},{16,17},{18,... | collective-permute-start | bytes 402488 | tf_op jit(solution)/shard_map/ppermute | solution.py:22
  42.2 7.4 %collective-permute-start.5 = (f32[1,258,130]{2,1,0:T(8,128)}, f32[1,258,130]{2,1,0:T(8,128)S(1)}, u32[]{:S(2)}, u32[]{:S(2)}) collective-permute-start(f32[1,258,130]{2,1,0:T(8,128)} %get-tuple-element.25), channel_id=1, source_target_pairs={{1,0},{3,2},{5,4},{7,6},{9,8},{11,10},{13,12},{15,14},{17,16},{19,... | collective-permute-start | bytes 402488 | tf_op jit(solution)/shard_map/ppermute | solution.py:23
  44.2 5.3 %collective-permute-start.10 = (f32[1,258,130]{2,1,0:T(8,128)S(1)}, f32[1,258,130]{2,1,0:T(8,128)S(1)}, u32[]{:S(2)}, u32[]{:S(2)}) collective-permute-start(f32[1,258,130]{2,1,0:T(8,128)S(1)} %get-tuple-element.27), channel_id=1, source_target_pairs={{0,1},{2,3},{4,5},{6,7},{8,9},{10,11},{12,13},{14,15},{16,17},{18,... | collective-permute-start | bytes 402488 | tf_op jit(solution)/shard_map/ppermute | solution.py:22
  46.9 4.1 %collective-permute-start.11 = (f32[1,258,130]{2,1,0:T(8,128)S(1)}, f32[1,258,130]{2,1,0:T(8,128)}, u32[]{:S(2)}, u32[]{:S(2)}) collective-permute-start(f32[1,258,130]{2,1,0:T(8,128)S(1)} %get-tuple-element.28), channel_id=1, source_target_pairs={{1,0},{3,2},{5,4},{7,6},{9,8},{11,10},{13,12},{15,14},{17,16},{19,... | collective-permute-start | bytes 402488 | tf_op jit(solution)/shard_map/ppermute | solution.py:23
  49.5 0.7 copy-start.18
  58.0 36.8 %copy-start = (f32[4,256,128]{2,1,0:T(8,128)}, f32[4,256,128]{2,1,0:T(8,128)S(1)}, u32[]{:S(2)}) copy-start(f32[4,256,128]{2,1,0:T(8,128)S(1)} %get-tuple-element.13) | copy-start | bytes 1572868
  58.1 36.8 %copy-start.9 = (f32[4,256,128]{2,1,0:T(8,128)}, f32[4,256,128]{2,1,0:T(8,128)S(1)}, u32[]{:S(2)}) copy-start(f32[4,256,128]{2,1,0:T(8,128)S(1)} %get-tuple-element.15) | copy-start | bytes 1572868
  58.1 36.8 %copy-start.11 = (f32[4,256,128]{2,1,0:T(8,128)}, f32[4,256,128]{2,1,0:T(8,128)S(1)}, u32[]{:S(2)}) copy-start(f32[4,256,128]{2,1,0:T(8,128)S(1)} %get-tuple-element.16) | copy-start | bytes 1572868
  60.0 14.9 %collective-permute-start.12 = (f32[4,256,1]{2,1,0:T(8,128)S(1)}, f32[4,256,1]{2,1,0:T(8,128)S(1)}, u32[]{:S(2)}, u32[]{:S(2)}) collective-permute-start(f32[4,256,1]{2,1,0:T(8,128)S(1)} %get-tuple-element.39), channel_id=1, source_target_pairs={{0,4},{4,8},{8,12},{1,5},{5,9},{9,13},{2,6},{6,10},{10,14},{3,7},{... | collective-permute-start | bytes 12296 | tf_op jit(solution)/shard_map/ppermute | solution.py:22
  63.5 16.1 %collective-permute-start.13 = (f32[4,256,1]{2,1,0:T(8,128)S(1)}, f32[4,256,1]{2,1,0:T(8,128)S(1)}, u32[]{:S(2)}, u32[]{:S(2)}) collective-permute-start(f32[4,256,1]{2,1,0:T(8,128)S(1)} %get-tuple-element.40), channel_id=1, source_target_pairs={{4,0},{8,4},{12,8},{5,1},{9,5},{13,9},{6,2},{10,6},{14,10},{7,3},{... | collective-permute-start | bytes 12296 | tf_op jit(solution)/shard_map/ppermute | solution.py:23
  79.7 5.9 %collective-permute-start.14 = (f32[4,1,130]{2,1,0:T(1,128)S(1)}, f32[4,1,130]{2,1,0:T(1,128)S(1)}, u32[]{:S(2)}, u32[]{:S(2)}) collective-permute-start(f32[4,1,130]{2,1,0:T(1,128)S(1)} %get-tuple-element.31), channel_id=1, source_target_pairs={{0,2},{1,3},{4,6},{5,7},{8,10},{9,11},{12,14},{13,15},{16,18},{17,... | collective-permute-start | bytes 6248 | tf_op jit(solution)/shard_map/ppermute | solution.py:22
  84.3 5.5 %collective-permute-start.15 = (f32[4,1,130]{2,1,0:T(1,128)S(1)}, f32[4,1,130]{2,1,0:T(1,128)S(1)}, u32[]{:S(2)}, u32[]{:S(2)}) collective-permute-start(f32[4,1,130]{2,1,0:T(1,128)S(1)} %get-tuple-element.32), channel_id=1, source_target_pairs={{2,0},{3,1},{6,4},{7,5},{10,8},{11,9},{14,12},{15,13},{18,16},{19,... | collective-permute-start | bytes 6248 | tf_op jit(solution)/shard_map/ppermute | solution.py:23
  90.1 2.6 %collective-permute-start.16 = (f32[1,258,130]{2,1,0:T(8,128)S(1)}, f32[1,258,130]{2,1,0:T(8,128)S(1)}, u32[]{:S(2)}, u32[]{:S(2)}) collective-permute-start(f32[1,258,130]{2,1,0:T(8,128)S(1)} %get-tuple-element.23), channel_id=1, source_target_pairs={{0,1},{2,3},{4,5},{6,7},{8,9},{10,11},{12,13},{14,15},{16,17},{18,... | collective-permute-start | bytes 402488 | tf_op jit(solution)/shard_map/ppermute | solution.py:22
  91.4 3.4 %collective-permute-start.17 = (f32[1,258,130]{2,1,0:T(8,128)S(1)}, f32[1,258,130]{2,1,0:T(8,128)S(1)}, u32[]{:S(2)}, u32[]{:S(2)}) collective-permute-start(f32[1,258,130]{2,1,0:T(8,128)S(1)} %get-tuple-element.24), channel_id=1, source_target_pairs={{1,0},{3,2},{5,4},{7,6},{9,8},{11,10},{13,12},{15,14},{17,16},{19,... | collective-permute-start | bytes 402488 | tf_op jit(solution)/shard_map/ppermute | solution.py:23
  96.6 0.8 copy-start.3
  133.2 29.1 %copy-start.6 = (f32[4,256,128]{2,1,0:T(8,128)}, f32[4,256,128]{2,1,0:T(8,128)S(1)}, u32[]{:S(2)}) copy-start(f32[4,256,128]{2,1,0:T(8,128)S(1)} %multiply_subtract_fusion.1) | copy-start | bytes 1572868
  133.4 12.6 %collective-permute-start.18 = (f32[4,256,1]{2,1,0:T(8,128)S(1)}, f32[4,256,1]{2,1,0:T(8,128)S(1)}, u32[]{:S(2)}, u32[]{:S(2)}) collective-permute-start(f32[4,256,1]{2,1,0:T(8,128)S(1)} %get-tuple-element.37), channel_id=1, source_target_pairs={{0,4},{4,8},{8,12},{1,5},{5,9},{9,13},{2,6},{6,10},{10,14},{3,7},{... | collective-permute-start | bytes 12296 | tf_op jit(solution)/shard_map/ppermute | solution.py:22
  134.7 15.5 %collective-permute-start.19 = (f32[4,256,1]{2,1,0:T(8,128)S(1)}, f32[4,256,1]{2,1,0:T(8,128)S(1)}, u32[]{:S(2)}, u32[]{:S(2)}) collective-permute-start(f32[4,256,1]{2,1,0:T(8,128)S(1)} %get-tuple-element.38), channel_id=1, source_target_pairs={{4,0},{8,4},{12,8},{5,1},{9,5},{13,9},{6,2},{10,6},{14,10},{7,3},{... | collective-permute-start | bytes 12296 | tf_op jit(solution)/shard_map/ppermute | solution.py:23
  150.3 2.8 %collective-permute-start.20 = (f32[4,1,130]{2,1,0:T(1,128)S(1)}, f32[4,1,130]{2,1,0:T(1,128)S(1)}, u32[]{:S(2)}, u32[]{:S(2)}) collective-permute-start(f32[4,1,130]{2,1,0:T(1,128)S(1)} %get-tuple-element.29), channel_id=1, source_target_pairs={{0,2},{1,3},{4,6},{5,7},{8,10},{9,11},{12,14},{13,15},{16,18},{17,... | collective-permute-start | bytes 6248 | tf_op jit(solution)/shard_map/ppermute | solution.py:22
  151.6 10.7 %copy-start.1 = (f32[4,256,128]{2,1,0:T(8,128)S(1)}, f32[4,256,128]{2,1,0:T(8,128)}, u32[]{:S(2)}) copy-start(f32[4,256,128]{2,1,0:T(8,128)} %copy-done) | copy-start | bytes 1572868
  151.6 10.7 %copy-start.4 = (f32[4,256,128]{2,1,0:T(8,128)S(1)}, f32[4,256,128]{2,1,0:T(8,128)}, u32[]{:S(2)}) copy-start(f32[4,256,128]{2,1,0:T(8,128)} %copy-done.3) | copy-start | bytes 1572868
  151.6 10.7 %copy-start.10 = (f32[4,256,128]{2,1,0:T(8,128)S(1)}, f32[4,256,128]{2,1,0:T(8,128)}, u32[]{:S(2)}) copy-start(f32[4,256,128]{2,1,0:T(8,128)} %copy-done.9) | copy-start | bytes 1572868
  151.6 10.7 %copy-start.12 = (f32[4,256,128]{2,1,0:T(8,128)S(1)}, f32[4,256,128]{2,1,0:T(8,128)}, u32[]{:S(2)}) copy-start(f32[4,256,128]{2,1,0:T(8,128)} %copy-done.11) | copy-start | bytes 1572868
  151.6 5.6 %collective-permute-start.21 = (f32[4,1,130]{2,1,0:T(1,128)S(1)}, f32[4,1,130]{2,1,0:T(1,128)S(1)}, u32[]{:S(2)}, u32[]{:S(2)}) collective-permute-start(f32[4,1,130]{2,1,0:T(1,128)S(1)} %get-tuple-element.30), channel_id=1, source_target_pairs={{2,0},{3,1},{6,4},{7,5},{10,8},{11,9},{14,12},{15,13},{18,16},{19,... | collective-permute-start | bytes 6248 | tf_op jit(solution)/shard_map/ppermute | solution.py:23
  157.5 2.6 %collective-permute-start.22 = (f32[1,258,130]{2,1,0:T(8,128)S(1)}, f32[1,258,130]{2,1,0:T(8,128)S(1)}, u32[]{:S(2)}, u32[]{:S(2)}) collective-permute-start(f32[1,258,130]{2,1,0:T(8,128)S(1)} %get-tuple-element.21), channel_id=1, source_target_pairs={{0,1},{2,3},{4,5},{6,7},{8,9},{10,11},{12,13},{14,15},{16,17},{18,... | collective-permute-start | bytes 402488 | tf_op jit(solution)/shard_map/ppermute | solution.py:22
  158.8 3.4 %collective-permute-start.23 = (f32[1,258,130]{2,1,0:T(8,128)S(1)}, f32[1,258,130]{2,1,0:T(8,128)S(1)}, u32[]{:S(2)}, u32[]{:S(2)}) collective-permute-start(f32[1,258,130]{2,1,0:T(8,128)S(1)} %get-tuple-element.22), channel_id=1, source_target_pairs={{1,0},{3,2},{5,4},{7,6},{9,8},{11,10},{13,12},{15,14},{17,16},{19,... | collective-permute-start | bytes 402488 | tf_op jit(solution)/shard_map/ppermute | solution.py:23
  199.4 2.2 %copy-start.2 = (f32[4,256,128]{2,1,0:T(8,128)S(1)}, f32[4,256,128]{2,1,0:T(8,128)}, u32[]{:S(2)}) copy-start(f32[4,256,128]{2,1,0:T(8,128)} %copy-done) | copy-start | bytes 1572868
  199.4 2.2 %copy-start.5 = (f32[4,256,128]{2,1,0:T(8,128)S(1)}, f32[4,256,128]{2,1,0:T(8,128)}, u32[]{:S(2)}) copy-start(f32[4,256,128]{2,1,0:T(8,128)} %copy-done.3) | copy-start | bytes 1572868
  199.4 2.2 %copy-start.17 = (f32[4,256,128]{2,1,0:T(8,128)S(1)}, f32[4,256,128]{2,1,0:T(8,128)}, u32[]{:S(2)}) copy-start(f32[4,256,128]{2,1,0:T(8,128)} %get-tuple-element.10) | copy-start | bytes 1572868
  (1 other events, 0.7 us)
where the time goes:
time: 203 us
  blocking collectives  60.5 us (30%)
  waiting for transfers between devices  54.7 us (27%)
  starting transfers between devices  49.4 us (24%)
  other arithmetic  23.4 us (12%)
  local copies, waits for them, and re-layouts  7.08 us (3%)
  between operations  6.83 us (3%)
    psum x2, blocking collectives, body(): lax.psum((jnp.sum(leftover_misfit * smoothed), jnp.sum(applied * smoothed...  60.5 us
    ppermute x12, starting transfers between devices, with_halo(): before = lax.ppermute(last, axis, up)  33.6 us
    ppermute x12, waiting for transfers between devices, with_halo(): after = lax.ppermute(first, axis, down)  30.7 us
    ppermute x12, waiting for transfers between devices, with_halo(): before = lax.ppermute(last, axis, up)  24.1 us
    ppermute x12, starting transfers between devices, with_halo(): after = lax.ppermute(first, axis, down)  15.8 us
    div x2, other arithmetic, smooth(): state = damping * vector / diagonal  7.15 us
    reduce_sum x2, other arithmetic, body(): jnp.sum(applied * smoothed)  4.26 us
  transfers between devices with their start and end apart: 24, of which 13 were waited for; matrix products, arithmetic and copies ran while one was open for 2% of the time, Pallas kernels for 0%

commit v1 on v0

--- a/solution.py
+++ b/solution.py
@@ -106,7 +106,10 @@
     applied = linear_map_action(smoothed)
     for turn in range(ITERS):
         gamma_now, delta_now = lax.psum(
-            (jnp.sum(leftover_misfit * smoothed), jnp.sum(applied * smoothed)), ("gx", "gy", "gz")
+            lax.psum(
+                (jnp.sum(leftover_misfit * smoothed), jnp.sum(applied * smoothed)), ("gy", "gz")
+            ),
+            "gx",
         )
         pre = smooth(applied)
         twice = linear_map_action(pre)

time: 203 us -> 175 us (0.86)
  blocking collectives: 60.5 us -> 32.8 us
  waiting for transfers between devices: 54.7 us -> 52.5 us
    psum x2, blocking collectives: 60.5 us -> 12.9 us  [body(): lax.psum((jnp.sum(leftover_misfit * smoothed), jnp.sum(applied * smoothed...]
    psum x0 -> x2, blocking collectives: none -> 19.8 us  [body(): lax.psum(lax.psum((jnp.sum(leftover_misfit * smoothed), jnp.sum(applied *...]
    ppermute x12, waiting for transfers between devices: 24.1 us -> 21.7 us  [with_halo(): before = lax.ppermute(last, axis, up)]
    ppermute x12, starting transfers between devices: 33.6 us -> 35.7 us  [with_halo(): before = lax.ppermute(last, axis, up)]
  transfers between devices with their start and end apart: 24 -> 24, of which waited for: 13 -> 13; matrix products, arithmetic and copies ran while one was open for 2% -> 3% of each run, Pallas kernels for 0% -> 0%
where the time goes in v1:
time: 175 us; the launch traced here: 174 us
  waiting for transfers between devices  52.5 us (30%)
  starting transfers between devices  51.4 us (29%)
  blocking collectives  32.8 us (19%)
  other arithmetic  23.3 us (13%)
  local copies, waits for them, and re-layouts  7.1 us (4%)
  between operations  6.95 us (4%)
    ppermute x12, starting transfers between devices, with_halo(): before = lax.ppermute(last, axis, up)  35.7 us
    ppermute x12, waiting for transfers between devices, with_halo(): after = lax.ppermute(first, axis, down)  30.7 us
    ppermute x12, waiting for transfers between devices, with_halo(): before = lax.ppermute(last, axis, up)  21.7 us
    psum x2, blocking collectives, body(): lax.psum(lax.psum((jnp.sum(leftover_misfit * smoothed), jnp.sum(applied *...  19.8 us
    ppermute x12, starting transfers between devices, with_halo(): after = lax.ppermute(first, axis, down)  15.8 us
    psum x2, blocking collectives, body(): lax.psum((jnp.sum(leftover_misfit * smoothed), jnp.sum(applied * smoothed...  12.9 us
    div x2, other arithmetic, smooth(): state = damping * vector / diagonal  6.98 us
    reduce_sum x2, other arithmetic, body(): jnp.sum(applied * smoothed)  4.24 us
  transfers between devices with their start and end apart: 24, of which 13 were waited for; matrix products, arithmetic and copies ran while one was open for 3% of the time, Pallas kernels for 0%

profile of v1, /device:TPU:0, one launch (start us, length us, event | category | flops | bytes accessed | tf_op | source)
XLA Modules:
  0.0 174.5 jit_solution(14735016677569949385)
XLA Ops:
  0.6 2.4 %fusion.120 = (f32[4,256,1]{2,1,0:T(8,128)}, f32[4,256,1]{2,1,0:T(8,128)}) fusion(f32[4,256,128]{2,1,0:T(8,128)} %param.10), kind=kLoop, calls=%fused_computation.277 | loop fusion | bytes 16384 | tf_op jit(solution)/shard_map/slice | solution.py:20
  3.0 5.0 %collective-permute-start = (f32[4,256,1]{2,1,0:T(8,128)}, f32[4,256,1]{2,1,0:T(8,128)S(1)}, u32[]{:S(2)}, u32[]{:S(2)}) collective-permute-start(f32[4,256,1]{2,1,0:T(8,128)} %get-tuple-element.45), channel_id=1, source_target_pairs={{0,4},{4,8},{8,12},{1,5},{5,9},{9,13},{2,6},{6,10},{10,14},{3,7},{... | collective-permute-start | bytes 12296 | tf_op jit(solution)/shard_map/ppermute | solution.py:22
  8.1 1.4 collective-permute-start.1
  9.5 1.1 fusion.121
  10.6 4.7 %collective-permute-start.6 = (f32[4,256,1]{2,1,0:T(8,128)}, f32[4,256,1]{2,1,0:T(8,128)S(1)}, u32[]{:S(2)}, u32[]{:S(2)}) collective-permute-start(f32[4,256,1]{2,1,0:T(8,128)} %get-tuple-element.47), channel_id=1, source_target_pairs={{0,4},{4,8},{8,12},{1,5},{5,9},{9,13},{2,6},{6,10},{10,14},{3,7},{... | collective-permute-start | bytes 12296 | tf_op jit(solution)/shard_map/ppermute | solution.py:22
  15.3 1.3 collective-permute-start.7
  17.5 3.1 %collective-permute-done = f32[4,256,1]{2,1,0:T(8,128)S(1)} collective-permute-done((f32[4,256,1]{2,1,0:T(8,128)}, f32[4,256,1]{2,1,0:T(8,128)S(1)}, u32[]{:S(2)}, u32[]{:S(2)}) %collective-permute-start) | collective-permute-done | bytes 4128 | tf_op jit(solution)/shard_map/ppermute | solution.py:22
  20.6 4.5 %collective-permute-done.1 = f32[4,256,1]{2,1,0:T(8,128)S(1)} collective-permute-done((f32[4,256,1]{2,1,0:T(8,128)}, f32[4,256,1]{2,1,0:T(8,128)S(1)}, u32[]{:S(2)}, u32[]{:S(2)}) %collective-permute-start.1) | collective-permute-done | bytes 4128 | tf_op jit(solution)/shard_map/ppermute | solution.py:23
  25.2 3.4 %collective-permute-start.2 = (f32[4,1,130]{2,1,0:T(1,128)S(1)}, f32[4,1,130]{2,1,0:T(1,128)S(1)}, u32[]{:S(2)}, u32[]{:S(2)}) collective-permute-start(f32[4,1,130]{2,1,0:T(1,128)S(1)} %get-tuple-element.37), channel_id=1, source_target_pairs={{0,2},{1,3},{4,6},{5,7},{8,10},{9,11},{12,14},{13,15},{16,18},{17,... | collective-permute-start | bytes 6248 | tf_op jit(solution)/shard_map/ppermute | solution.py:22
  28.6 1.3 collective-permute-start.3
  30.7 4.2 %collective-permute-done.7 = f32[4,256,1]{2,1,0:T(8,128)S(1)} collective-permute-done((f32[4,256,1]{2,1,0:T(8,128)}, f32[4,256,1]{2,1,0:T(8,128)S(1)}, u32[]{:S(2)}, u32[]{:S(2)}) %collective-permute-start.7) | collective-permute-done | bytes 4128 | tf_op jit(solution)/shard_map/ppermute | solution.py:23
  35.0 3.4 %collective-permute-start.8 = (f32[4,1,130]{2,1,0:T(1,128)S(1)}, f32[4,1,130]{2,1,0:T(1,128)S(1)}, u32[]{:S(2)}, u32[]{:S(2)}) collective-permute-start(f32[4,1,130]{2,1,0:T(1,128)S(1)} %get-tuple-element.39), channel_id=1, source_target_pairs={{0,2},{1,3},{4,6},{5,7},{8,10},{9,11},{12,14},{13,15},{16,18},{17,... | collective-permute-start | bytes 6248 | tf_op jit(solution)/shard_map/ppermute | solution.py:22
  38.4 1.3 collective-permute-start.9
  39.8 1.1 pad_maximum_fusion.87
  40.9 1.3 collective-permute-start.4
  42.2 1.3 collective-permute-start.5
  44.2 2.6 %collective-permute-start.10 = (f32[1,258,130]{2,1,0:T(8,128)S(1)}, f32[1,258,130]{2,1,0:T(8,128)S(1)}, u32[]{:S(2)}, u32[]{:S(2)}) collective-permute-start(f32[1,258,130]{2,1,0:T(8,128)S(1)} %get-tuple-element.31), channel_id=1, source_target_pairs={{0,1},{2,3},{4,5},{6,7},{8,9},{10,11},{12,13},{14,15},{16,17},{18,... | collective-permute-start | bytes 402488 | tf_op jit(solution)/shard_map/ppermute | solution.py:22
  46.9 1.3 collective-permute-start.11
  51.0 6.9 %multiply_divide_fusion.1 = (f32[4,256,128]{2,1,0:T(8,128)S(1)}, f32[4,256,128]{2,1,0:T(8,128)S(1)}, f32[4,256,128]{2,1,0:T(8,128)S(1)}, f32[4,256,128]{2,1,0:T(...) fusion(f32[4,256,1]{2,1,0:T(8,128)} %copy-done.16, ...), kind=kLoop, calls=%fused_computation.215 | loop fusion | flops 10878976 | bytes 7381184 | tf_op jit(solution)/shard_map/div | solution.py:92
  59.9 3.5 %collective-permute-start.12 = (f32[4,256,1]{2,1,0:T(8,128)S(1)}, f32[4,256,1]{2,1,0:T(8,128)S(1)}, u32[]{:S(2)}, u32[]{:S(2)}) collective-permute-start(f32[4,256,1]{2,1,0:T(8,128)S(1)} %get-tuple-element.43), channel_id=1, source_target_pairs={{0,4},{4,8},{8,12},{1,5},{5,9},{9,13},{2,6},{6,10},{10,14},{3,7},{... | collective-permute-start | bytes 12296 | tf_op jit(solution)/shard_map/ppermute | solution.py:22
  63.3 1.3 collective-permute-start.13
  64.6 10.1 %collective-permute-done.12 = f32[4,256,1]{2,1,0:T(8,128)S(1)} collective-permute-done((f32[4,256,1]{2,1,0:T(8,128)S(1)}, f32[4,256,1]{2,1,0:T(8,128)S(1)}, u32[]{:S(2)}, u32[]{:S(2)}) %collective-permute-start.12) | collective-permute-done | bytes 4128 | tf_op jit(solution)/shard_map/ppermute | solution.py:22
  74.8 4.7 %collective-permute-done.13 = f32[4,256,1]{2,1,0:T(8,128)S(1)} collective-permute-done((f32[4,256,1]{2,1,0:T(8,128)S(1)}, f32[4,256,1]{2,1,0:T(8,128)S(1)}, u32[]{:S(2)}, u32[]{:S(2)}) %collective-permute-start.13) | collective-permute-done | bytes 4128 | tf_op jit(solution)/shard_map/ppermute | solution.py:23
  79.6 4.5 %collective-permute-start.14 = (f32[4,1,130]{2,1,0:T(1,128)S(1)}, f32[4,1,130]{2,1,0:T(1,128)S(1)}, u32[]{:S(2)}, u32[]{:S(2)}) collective-permute-start(f32[4,1,130]{2,1,0:T(1,128)S(1)} %get-tuple-element.35), channel_id=1, source_target_pairs={{0,2},{1,3},{4,6},{5,7},{8,10},{9,11},{12,14},{13,15},{16,18},{17,... | collective-permute-start | bytes 6248 | tf_op jit(solution)/shard_map/ppermute | solution.py:22
  84.1 1.3 collective-permute-start.15
  85.4 4.2 %collective-permute-done.15 = f32[4,1,130]{2,1,0:T(1,128)S(1)} collective-permute-done((f32[4,1,130]{2,1,0:T(1,128)S(1)}, f32[4,1,130]{2,1,0:T(1,128)S(1)}, u32[]{:S(2)}, u32[]{:S(2)}) %collective-permute-start.15) | collective-permute-done | bytes 2112 | tf_op jit(solution)/shard_map/ppermute | solution.py:23
  89.9 1.3 collective-permute-start.16
  91.2 1.3 collective-permute-start.17
  92.5 2.1 %collective-permute-done.17 = f32[1,258,130]{2,1,0:T(8,128)S(1)} collective-permute-done((f32[1,258,130]{2,1,0:T(8,128)S(1)}, f32[1,258,130]{2,1,0:T(8,128)S(1)}, u32[]{:S(2)}, u32[]{:S(2)}) %collective-permute-start.17) | collective-permute-done | bytes 134192 | tf_op jit(solution)/shard_map/ppermute | solution.py:23
  94.7 1.8 %multiply_reduce_fusion.2 = (f32[]{:T(128)}, f32[]{:T(128)}, f32[4,256,128]{2,1,0:T(8,128)S(1)}) fusion(f32[4,256,128]{2,1,0:T(8,128)S(1)} %fusion.32, f32[4,256,128]{2,1,0:T(8,128)S(1)} %get-tuple-element.17, f32[4,256,128]{2,1,0:T(8,128)S(1)} %get-tuple-element.24, f32[4,256,1]{2,1,0:T(8,128)S(1)} %collective-permute-done.13, ...), kind=kLoop, calls=%fused_computation.213 | loop fusion | flops 4587518 | bytes 5523560 | tf_op jit(solution)/shard_map/reduce_sum | solution.py:110
  97.2 1.4 fusion.56
  98.6 6.5 %all-reduce.7 = (f32[]{:T(128)}, f32[]{:T(128)}) all-reduce(f32[]{:T(128)} %get-tuple-element.5, f32[]{:T(128)} %get-tuple-element.4), channel_id=1, replica_groups=mesh['groups'=2,'gx'=4,'gy'=2,'gz'=2] {'gy','gz'}, use_global_device_ids=true, to_apply=%region_1.2 | all-reduce | flops 2 | bytes 16 | tf_op jit(solution)/shard_map/psum | solution.py:109
  105.1 10.6 %all-reduce.9 = (f32[]{:T(128)}, f32[]{:T(128)}) all-reduce(f32[]{:T(128)} %get-tuple-element.8, f32[]{:T(128)} %get-tuple-element.9), channel_id=1, replica_groups=mesh['groups'=2,'gx'=4,'gy'=2,'gz'=2] {'gx'}, use_global_device_ids=true, to_apply=%region_2.3 | all-reduce | flops 2 | bytes 16 | tf_op jit(solution)/shard_map/psum | solution.py:108
  117.0 2.9 %multiply_subtract_fusion.1 = f32[4,256,128]{2,1,0:T(8,128)S(1)} fusion(f32[4,256,128]{2,1,0:T(8,128)S(1)} %fusion.32, f32[4,256,128]{2,1,0:T(8,128)} %fusion.56, f32[4,256,128]{2,1,0:T(8,128)S(1)} %get-tuple-element.18, f32[4,256,128]{2,1,0:T(8,128)} %copy-done.3, f32[4,256,128]{2,1,0:T(8,128)S(1)} %get-tuple-element.24, ...), kind=kLoop, calls=%fused_computation.210 | loop fusion | flops 2490368 | bytes 4722692 | tf_op jit(solution)/shard_map/sub | solution.py:136
  120.1 2.4 %collective-permute-start.18 = (f32[4,256,1]{2,1,0:T(8,128)S(1)}, f32[4,256,1]{2,1,0:T(8,128)S(1)}, u32[]{:S(2)}, u32[]{:S(2)}) collective-permute-start(f32[4,256,1]{2,1,0:T(8,128)S(1)} %get-tuple-element.41), channel_id=1, source_target_pairs={{0,4},{4,8},{8,12},{1,5},{5,9},{9,13},{2,6},{6,10},{10,14},{3,7},{... | collective-permute-start | bytes 12296 | tf_op jit(solution)/shard_map/ppermute | solution.py:22
  122.5 1.3 collective-permute-start.19
  123.8 7.7 %collective-permute-done.18 = f32[4,256,1]{2,1,0:T(8,128)S(1)} collective-permute-done((f32[4,256,1]{2,1,0:T(8,128)S(1)}, f32[4,256,1]{2,1,0:T(8,128)S(1)}, u32[]{:S(2)}, u32[]{:S(2)}) %collective-permute-start.18) | collective-permute-done | bytes 4128 | tf_op jit(solution)/shard_map/ppermute | solution.py:22
  131.5 4.1 %collective-permute-done.19 = f32[4,256,1]{2,1,0:T(8,128)S(1)} collective-permute-done((f32[4,256,1]{2,1,0:T(8,128)S(1)}, f32[4,256,1]{2,1,0:T(8,128)S(1)}, u32[]{:S(2)}, u32[]{:S(2)}) %collective-permute-start.19) | collective-permute-done | bytes 4128 | tf_op jit(solution)/shard_map/ppermute | solution.py:23
  135.8 2.3 %collective-permute-start.20 = (f32[4,1,130]{2,1,0:T(1,128)S(1)}, f32[4,1,130]{2,1,0:T(1,128)S(1)}, u32[]{:S(2)}, u32[]{:S(2)}) collective-permute-start(f32[4,1,130]{2,1,0:T(1,128)S(1)} %get-tuple-element.33), channel_id=1, source_target_pairs={{0,2},{1,3},{4,6},{5,7},{8,10},{9,11},{12,14},{13,15},{16,18},{17,... | collective-permute-start | bytes 6248 | tf_op jit(solution)/shard_map/ppermute | solution.py:22
  138.1 1.4 collective-permute-start.21
  139.6 4.2 %collective-permute-done.21 = f32[4,1,130]{2,1,0:T(1,128)S(1)} collective-permute-done((f32[4,1,130]{2,1,0:T(1,128)S(1)}, f32[4,1,130]{2,1,0:T(1,128)S(1)}, u32[]{:S(2)}, u32[]{:S(2)}) %collective-permute-start.21) | collective-permute-done | bytes 2112 | tf_op jit(solution)/shard_map/ppermute | solution.py:23
  144.0 1.3 collective-permute-start.22
  145.3 1.3 collective-permute-start.23
  146.7 2.1 %collective-permute-done.23 = f32[1,258,130]{2,1,0:T(8,128)S(1)} collective-permute-done((f32[1,258,130]{2,1,0:T(8,128)S(1)}, f32[1,258,130]{2,1,0:T(8,128)S(1)}, u32[]{:S(2)}, u32[]{:S(2)}) %collective-permute-start.23) | collective-permute-done | bytes 134192 | tf_op jit(solution)/shard_map/ppermute | solution.py:23
  148.8 2.5 %multiply_reduce_fusion = (f32[]{:T(128)}, f32[]{:T(128)}, f32[4,256,128]{2,1,0:T(8,128)}) fusion(f32[4,256,128]{2,1,0:T(8,128)S(1)} %multiply_subtract_fusion.1, f32[4,256,128]{2,1,0:T(8,128)S(1)} %copy-done.1, f32[4,256,128]{2,1,0:T(8,128)S(1)} %copy-done.4, f32[]{:T(128)S(6)} %div.69, f32[4,256,128]{2,1,0:T(8,128)S(1)} %get-tuple-element.24, ...), kind=kLoop, calls=%fused_computation.208 | loop fusion | flops 4849662 | bytes 6047852 | tf_op jit(solution)/shard_map/reduce_sum | solution.py:110
  151.3 6.5 %all-reduce.6 = (f32[]{:T(128)}, f32[]{:T(128)}) all-reduce(f32[]{:T(128)} %get-tuple-element.3, f32[]{:T(128)} %get-tuple-element.2), channel_id=1, replica_groups=mesh['groups'=2,'gx'=4,'gy'=2,'gz'=2] {'gy','gz'}, use_global_device_ids=true, to_apply=%region_7.8 | all-reduce | flops 2 | bytes 16 | tf_op jit(solution)/shard_map/psum | solution.py:109
  157.7 9.2 %all-reduce.8 = (f32[]{:T(128)}, f32[]{:T(128)}) all-reduce(f32[]{:T(128)} %get-tuple-element.6, f32[]{:T(128)} %get-tuple-element.7), channel_id=1, replica_groups=mesh['groups'=2,'gx'=4,'gy'=2,'gz'=2] {'gx'}, use_global_device_ids=true, to_apply=%region_8.9 | all-reduce | flops 2 | bytes 16 | tf_op jit(solution)/shard_map/psum | solution.py:108
  171.4 2.2 %multiply_add_fusion = f32[4,256,128]{2,1,0:T(8,128)} fusion(f32[4,256,128]{2,1,0:T(8,128)} %copy-done.6, f32[4,256,128]{2,1,0:T(8,128)S(1)} %fusion.32, f32[4,256,128]{2,1,0:T(8,128)} %param.8, f32[]{:T(128)S(6)} %div.74, f32[]{:T(128)S(6)} %div.76, f32[]{:T(128)S(6)} %div.69), kind=kLoop, calls=%fused_computation.207 | loop fusion | flops 786432 | bytes 2097164 | tf_op jit(solution)/shard_map/add | solution.py:133
  (96 shorter events, 10.0 us)
Async XLA Ops:
  0.6 8.9 %copy-start.7 = (f32[4,256,128]{2,1,0:T(8,128)S(1)}, f32[4,256,128]{2,1,0:T(8,128)}, u32[]{:S(2)}) copy-start(f32[4,256,128]{2,1,0:T(8,128)} %param.8) | copy-start | bytes 1572868
  3.0 17.6 %collective-permute-start = (f32[4,256,1]{2,1,0:T(8,128)}, f32[4,256,1]{2,1,0:T(8,128)S(1)}, u32[]{:S(2)}, u32[]{:S(2)}) collective-permute-start(f32[4,256,1]{2,1,0:T(8,128)} %get-tuple-element.45), channel_id=1, source_target_pairs={{0,4},{4,8},{8,12},{1,5},{5,9},{9,13},{2,6},{6,10},{10,14},{3,7},{... | collective-permute-start | bytes 12296 | tf_op jit(solution)/shard_map/ppermute | solution.py:22
  8.0 8.6 %copy-start.23 = (s32[4,1]{0,1:T(1,128)S(1)}, s32[4,1]{0,1:T(1,128)}, u32[]{:S(2)}) copy-start(s32[4,1]{0,1:T(1,128)} %param.14) | copy-start | bytes 52
  8.0 8.8 %copy-start.24 = (s32[4]{0:T(128)S(1)}, s32[4]{0:T(128)}, u32[]{:S(2)}) copy-start(s32[4]{0:T(128)} %param.15) | copy-start | bytes 52
  8.0 8.8 %copy-start.22 = (s32[4,4,1]{1,2,0:T(1,128)S(1)}, s32[4,4,1]{1,2,0:T(1,128)}, u32[]{:S(2)}) copy-start(s32[4,4,1]{1,2,0:T(1,128)} %param.13) | copy-start | bytes 196
  8.1 8.8 %copy-start.20 = (f32[8,64,128]{2,1,0:T(8,128)S(1)}, f32[8,64,128]{2,1,0:T(8,128)}, u32[]{:S(2)}) copy-start(f32[8,64,128]{2,1,0:T(8,128)} %param.11) | copy-start | bytes 786436
  8.1 8.8 %copy-start.21 = (s32[4,4,1]{1,2,0:T(1,128)S(1)}, s32[4,4,1]{1,2,0:T(1,128)}, u32[]{:S(2)}) copy-start(s32[4,4,1]{1,2,0:T(1,128)} %param.12) | copy-start | bytes 196
  8.1 17.0 %collective-permute-start.1 = (f32[4,256,1]{2,1,0:T(8,128)}, f32[4,256,1]{2,1,0:T(8,128)S(1)}, u32[]{:S(2)}, u32[]{:S(2)}) collective-permute-start(f32[4,256,1]{2,1,0:T(8,128)} %get-tuple-element.46), channel_id=1, source_target_pairs={{4,0},{8,4},{12,8},{5,1},{9,5},{13,9},{6,2},{10,6},{14,10},{7,3},{... | collective-permute-start | bytes 12296 | tf_op jit(solution)/shard_map/ppermute | solution.py:23
  10.6 14.5 %copy-start.8 = (f32[4,256,128]{2,1,0:T(8,128)S(1)}, f32[4,256,128]{2,1,0:T(8,128)}, u32[]{:S(2)}) copy-start(f32[4,256,128]{2,1,0:T(8,128)} %param.10) | copy-start | bytes 1572868
  10.6 20.1 %collective-permute-start.6 = (f32[4,256,1]{2,1,0:T(8,128)}, f32[4,256,1]{2,1,0:T(8,128)S(1)}, u32[]{:S(2)}, u32[]{:S(2)}) collective-permute-start(f32[4,256,1]{2,1,0:T(8,128)} %get-tuple-element.47), channel_id=1, source_target_pairs={{0,4},{4,8},{8,12},{1,5},{5,9},{9,13},{2,6},{6,10},{10,14},{3,7},{... | collective-permute-start | bytes 12296 | tf_op jit(solution)/shard_map/ppermute | solution.py:22
  15.3 19.6 %collective-permute-start.7 = (f32[4,256,1]{2,1,0:T(8,128)}, f32[4,256,1]{2,1,0:T(8,128)S(1)}, u32[]{:S(2)}, u32[]{:S(2)}) collective-permute-start(f32[4,256,1]{2,1,0:T(8,128)} %get-tuple-element.48), channel_id=1, source_target_pairs={{4,0},{8,4},{12,8},{5,1},{9,5},{13,9},{6,2},{10,6},{14,10},{7,3},{... | collective-permute-start | bytes 12296 | tf_op jit(solution)/shard_map/ppermute | solution.py:23
  20.6 19.2 %copy-start.13 = (f32[4,256,1]{2,1,0:T(8,128)}, f32[4,256,1]{2,1,0:T(8,128)S(1)}, u32[]{:S(2)}) copy-start(f32[4,256,1]{2,1,0:T(8,128)S(1)} %collective-permute-done) | copy-start | bytes 12292
  25.1 14.7 %copy-start.14 = (f32[4,256,1]{2,1,0:T(8,128)}, f32[4,256,1]{2,1,0:T(8,128)S(1)}, u32[]{:S(2)}) copy-start(f32[4,256,1]{2,1,0:T(8,128)S(1)} %collective-permute-done.1) | copy-start | bytes 12292
  25.2 14.5 %collective-permute-start.2 = (f32[4,1,130]{2,1,0:T(1,128)S(1)}, f32[4,1,130]{2,1,0:T(1,128)S(1)}, u32[]{:S(2)}, u32[]{:S(2)}) collective-permute-start(f32[4,1,130]{2,1,0:T(1,128)S(1)} %get-tuple-element.37), channel_id=1, source_target_pairs={{0,2},{1,3},{4,6},{5,7},{8,10},{9,11},{12,14},{13,15},{16,18},{17,... | collective-permute-start | bytes 6248 | tf_op jit(solution)/shard_map/ppermute | solution.py:22
  28.6 11.1 %collective-permute-start.3 = (f32[4,1,130]{2,1,0:T(1,128)S(1)}, f32[4,1,130]{2,1,0:T(1,128)S(1)}, u32[]{:S(2)}, u32[]{:S(2)}) collective-permute-start(f32[4,1,130]{2,1,0:T(1,128)S(1)} %get-tuple-element.38), channel_id=1, source_target_pairs={{2,0},{3,1},{6,4},{7,5},{10,8},{11,9},{14,12},{15,13},{18,16},{19,... | collective-permute-start | bytes 6248 | tf_op jit(solution)/shard_map/ppermute | solution.py:23
  30.7 13.2 %copy-start.15 = (f32[4,256,1]{2,1,0:T(8,128)}, f32[4,256,1]{2,1,0:T(8,128)S(1)}, u32[]{:S(2)}) copy-start(f32[4,256,1]{2,1,0:T(8,128)S(1)} %collective-permute-done.6) | copy-start | bytes 12292
  34.9 9.0 %copy-start.16 = (f32[4,256,1]{2,1,0:T(8,128)}, f32[4,256,1]{2,1,0:T(8,128)S(1)}, u32[]{:S(2)}) copy-start(f32[4,256,1]{2,1,0:T(8,128)S(1)} %collective-permute-done.7) | copy-start | bytes 12292
  35.0 8.4 %collective-permute-start.8 = (f32[4,1,130]{2,1,0:T(1,128)S(1)}, f32[4,1,130]{2,1,0:T(1,128)S(1)}, u32[]{:S(2)}, u32[]{:S(2)}) collective-permute-start(f32[4,1,130]{2,1,0:T(1,128)S(1)} %get-tuple-element.39), channel_id=1, source_target_pairs={{0,2},{1,3},{4,6},{5,7},{8,10},{9,11},{12,14},{13,15},{16,18},{17,... | collective-permute-start | bytes 6248 | tf_op jit(solution)/shard_map/ppermute | solution.py:22
  38.4 5.5 %collective-permute-start.9 = (f32[4,1,130]{2,1,0:T(1,128)S(1)}, f32[4,1,130]{2,1,0:T(1,128)S(1)}, u32[]{:S(2)}, u32[]{:S(2)}) collective-permute-start(f32[4,1,130]{2,1,0:T(1,128)S(1)} %get-tuple-element.40), channel_id=1, source_target_pairs={{2,0},{3,1},{6,4},{7,5},{10,8},{11,9},{14,12},{15,13},{18,16},{19,... | collective-permute-start | bytes 6248 | tf_op jit(solution)/shard_map/ppermute | solution.py:23
  40.9 8.7 %collective-permute-start.4 = (f32[1,258,130]{2,1,0:T(8,128)}, f32[1,258,130]{2,1,0:T(8,128)S(1)}, u32[]{:S(2)}, u32[]{:S(2)}) collective-permute-start(f32[1,258,130]{2,1,0:T(8,128)} %get-tuple-element.30), channel_id=1, source_target_pairs={{0,1},{2,3},{4,5},{6,7},{8,9},{10,11},{12,13},{14,15},{16,17},{18,... | collective-permute-start | bytes 402488 | tf_op jit(solution)/shard_map/ppermute | solution.py:22
  42.2 7.4 %collective-permute-start.5 = (f32[1,258,130]{2,1,0:T(8,128)}, f32[1,258,130]{2,1,0:T(8,128)S(1)}, u32[]{:S(2)}, u32[]{:S(2)}) collective-permute-start(f32[1,258,130]{2,1,0:T(8,128)} %get-tuple-element.29), channel_id=1, source_target_pairs={{1,0},{3,2},{5,4},{7,6},{9,8},{11,10},{13,12},{15,14},{17,16},{19,... | collective-permute-start | bytes 402488 | tf_op jit(solution)/shard_map/ppermute | solution.py:23
  44.2 5.3 %collective-permute-start.10 = (f32[1,258,130]{2,1,0:T(8,128)S(1)}, f32[1,258,130]{2,1,0:T(8,128)S(1)}, u32[]{:S(2)}, u32[]{:S(2)}) collective-permute-start(f32[1,258,130]{2,1,0:T(8,128)S(1)} %get-tuple-element.31), channel_id=1, source_target_pairs={{0,1},{2,3},{4,5},{6,7},{8,9},{10,11},{12,13},{14,15},{16,17},{18,... | collective-permute-start | bytes 402488 | tf_op jit(solution)/shard_map/ppermute | solution.py:22
  46.9 4.1 %collective-permute-start.11 = (f32[1,258,130]{2,1,0:T(8,128)S(1)}, f32[1,258,130]{2,1,0:T(8,128)}, u32[]{:S(2)}, u32[]{:S(2)}) collective-permute-start(f32[1,258,130]{2,1,0:T(8,128)S(1)} %get-tuple-element.32), channel_id=1, source_target_pairs={{1,0},{3,2},{5,4},{7,6},{9,8},{11,10},{13,12},{15,14},{17,16},{19,... | collective-permute-start | bytes 402488 | tf_op jit(solution)/shard_map/ppermute | solution.py:23
  49.5 0.7 copy-start.18
  57.9 36.8 %copy-start = (f32[4,256,128]{2,1,0:T(8,128)}, f32[4,256,128]{2,1,0:T(8,128)S(1)}, u32[]{:S(2)}) copy-start(f32[4,256,128]{2,1,0:T(8,128)S(1)} %get-tuple-element.17) | copy-start | bytes 1572868
  57.9 36.8 %copy-start.9 = (f32[4,256,128]{2,1,0:T(8,128)}, f32[4,256,128]{2,1,0:T(8,128)S(1)}, u32[]{:S(2)}) copy-start(f32[4,256,128]{2,1,0:T(8,128)S(1)} %get-tuple-element.19) | copy-start | bytes 1572868
  57.9 36.8 %copy-start.11 = (f32[4,256,128]{2,1,0:T(8,128)}, f32[4,256,128]{2,1,0:T(8,128)S(1)}, u32[]{:S(2)}) copy-start(f32[4,256,128]{2,1,0:T(8,128)S(1)} %get-tuple-element.20) | copy-start | bytes 1572868
  59.9 14.9 %collective-permute-start.12 = (f32[4,256,1]{2,1,0:T(8,128)S(1)}, f32[4,256,1]{2,1,0:T(8,128)S(1)}, u32[]{:S(2)}, u32[]{:S(2)}) collective-permute-start(f32[4,256,1]{2,1,0:T(8,128)S(1)} %get-tuple-element.43), channel_id=1, source_target_pairs={{0,4},{4,8},{8,12},{1,5},{5,9},{9,13},{2,6},{6,10},{10,14},{3,7},{... | collective-permute-start | bytes 12296 | tf_op jit(solution)/shard_map/ppermute | solution.py:22
  63.3 16.1 %collective-permute-start.13 = (f32[4,256,1]{2,1,0:T(8,128)S(1)}, f32[4,256,1]{2,1,0:T(8,128)S(1)}, u32[]{:S(2)}, u32[]{:S(2)}) collective-permute-start(f32[4,256,1]{2,1,0:T(8,128)S(1)} %get-tuple-element.44), channel_id=1, source_target_pairs={{4,0},{8,4},{12,8},{5,1},{9,5},{13,9},{6,2},{10,6},{14,10},{7,3},{... | collective-permute-start | bytes 12296 | tf_op jit(solution)/shard_map/ppermute | solution.py:23
  79.6 5.9 %collective-permute-start.14 = (f32[4,1,130]{2,1,0:T(1,128)S(1)}, f32[4,1,130]{2,1,0:T(1,128)S(1)}, u32[]{:S(2)}, u32[]{:S(2)}) collective-permute-start(f32[4,1,130]{2,1,0:T(1,128)S(1)} %get-tuple-element.35), channel_id=1, source_target_pairs={{0,2},{1,3},{4,6},{5,7},{8,10},{9,11},{12,14},{13,15},{16,18},{17,... | collective-permute-start | bytes 6248 | tf_op jit(solution)/shard_map/ppermute | solution.py:22
  84.1 5.5 %collective-permute-start.15 = (f32[4,1,130]{2,1,0:T(1,128)S(1)}, f32[4,1,130]{2,1,0:T(1,128)S(1)}, u32[]{:S(2)}, u32[]{:S(2)}) collective-permute-start(f32[4,1,130]{2,1,0:T(1,128)S(1)} %get-tuple-element.36), channel_id=1, source_target_pairs={{2,0},{3,1},{6,4},{7,5},{10,8},{11,9},{14,12},{15,13},{18,16},{19,... | collective-permute-start | bytes 6248 | tf_op jit(solution)/shard_map/ppermute | solution.py:23
  89.9 2.6 %collective-permute-start.16 = (f32[1,258,130]{2,1,0:T(8,128)S(1)}, f32[1,258,130]{2,1,0:T(8,128)S(1)}, u32[]{:S(2)}, u32[]{:S(2)}) collective-permute-start(f32[1,258,130]{2,1,0:T(8,128)S(1)} %get-tuple-element.27), channel_id=1, source_target_pairs={{0,1},{2,3},{4,5},{6,7},{8,9},{10,11},{12,13},{14,15},{16,17},{18,... | collective-permute-start | bytes 402488 | tf_op jit(solution)/shard_map/ppermute | solution.py:22
  91.2 3.4 %collective-permute-start.17 = (f32[1,258,130]{2,1,0:T(8,128)S(1)}, f32[1,258,130]{2,1,0:T(8,128)S(1)}, u32[]{:S(2)}, u32[]{:S(2)}) collective-permute-start(f32[1,258,130]{2,1,0:T(8,128)S(1)} %get-tuple-element.28), channel_id=1, source_target_pairs={{1,0},{3,2},{5,4},{7,6},{9,8},{11,10},{13,12},{15,14},{17,16},{19,... | collective-permute-start | bytes 402488 | tf_op jit(solution)/shard_map/ppermute | solution.py:23
  96.4 0.8 copy-start.3
  119.9 28.9 %copy-start.6 = (f32[4,256,128]{2,1,0:T(8,128)}, f32[4,256,128]{2,1,0:T(8,128)S(1)}, u32[]{:S(2)}) copy-start(f32[4,256,128]{2,1,0:T(8,128)S(1)} %multiply_subtract_fusion.1) | copy-start | bytes 1572868
  120.1 11.4 %collective-permute-start.18 = (f32[4,256,1]{2,1,0:T(8,128)S(1)}, f32[4,256,1]{2,1,0:T(8,128)S(1)}, u32[]{:S(2)}, u32[]{:S(2)}) collective-permute-start(f32[4,256,1]{2,1,0:T(8,128)S(1)} %get-tuple-element.41), channel_id=1, source_target_pairs={{0,4},{4,8},{8,12},{1,5},{5,9},{9,13},{2,6},{6,10},{10,14},{3,7},{... | collective-permute-start | bytes 12296 | tf_op jit(solution)/shard_map/ppermute | solution.py:22
  122.5 13.2 %collective-permute-start.19 = (f32[4,256,1]{2,1,0:T(8,128)S(1)}, f32[4,256,1]{2,1,0:T(8,128)S(1)}, u32[]{:S(2)}, u32[]{:S(2)}) collective-permute-start(f32[4,256,1]{2,1,0:T(8,128)S(1)} %get-tuple-element.42), channel_id=1, source_target_pairs={{4,0},{8,4},{12,8},{5,1},{9,5},{13,9},{6,2},{10,6},{14,10},{7,3},{... | collective-permute-start | bytes 12296 | tf_op jit(solution)/shard_map/ppermute | solution.py:23
  135.8 3.8 %collective-permute-start.20 = (f32[4,1,130]{2,1,0:T(1,128)S(1)}, f32[4,1,130]{2,1,0:T(1,128)S(1)}, u32[]{:S(2)}, u32[]{:S(2)}) collective-permute-start(f32[4,1,130]{2,1,0:T(1,128)S(1)} %get-tuple-element.33), channel_id=1, source_target_pairs={{0,2},{1,3},{4,6},{5,7},{8,10},{9,11},{12,14},{13,15},{16,18},{17,... | collective-permute-start | bytes 6248 | tf_op jit(solution)/shard_map/ppermute | solution.py:22
  138.1 10.7 %copy-start.1 = (f32[4,256,128]{2,1,0:T(8,128)S(1)}, f32[4,256,128]{2,1,0:T(8,128)}, u32[]{:S(2)}) copy-start(f32[4,256,128]{2,1,0:T(8,128)} %copy-done) | copy-start | bytes 1572868
  138.1 10.7 %copy-start.4 = (f32[4,256,128]{2,1,0:T(8,128)S(1)}, f32[4,256,128]{2,1,0:T(8,128)}, u32[]{:S(2)}) copy-start(f32[4,256,128]{2,1,0:T(8,128)} %copy-done.3) | copy-start | bytes 1572868
  138.1 10.7 %copy-start.10 = (f32[4,256,128]{2,1,0:T(8,128)S(1)}, f32[4,256,128]{2,1,0:T(8,128)}, u32[]{:S(2)}) copy-start(f32[4,256,128]{2,1,0:T(8,128)} %copy-done.9) | copy-start | bytes 1572868
  138.1 10.7 %copy-start.12 = (f32[4,256,128]{2,1,0:T(8,128)S(1)}, f32[4,256,128]{2,1,0:T(8,128)}, u32[]{:S(2)}) copy-start(f32[4,256,128]{2,1,0:T(8,128)} %copy-done.11) | copy-start | bytes 1572868
  138.1 5.6 %collective-permute-start.21 = (f32[4,1,130]{2,1,0:T(1,128)S(1)}, f32[4,1,130]{2,1,0:T(1,128)S(1)}, u32[]{:S(2)}, u32[]{:S(2)}) collective-permute-start(f32[4,1,130]{2,1,0:T(1,128)S(1)} %get-tuple-element.34), channel_id=1, source_target_pairs={{2,0},{3,1},{6,4},{7,5},{10,8},{11,9},{14,12},{15,13},{18,16},{19,... | collective-permute-start | bytes 6248 | tf_op jit(solution)/shard_map/ppermute | solution.py:23
  144.0 2.6 %collective-permute-start.22 = (f32[1,258,130]{2,1,0:T(8,128)S(1)}, f32[1,258,130]{2,1,0:T(8,128)S(1)}, u32[]{:S(2)}, u32[]{:S(2)}) collective-permute-start(f32[1,258,130]{2,1,0:T(8,128)S(1)} %get-tuple-element.25), channel_id=1, source_target_pairs={{0,1},{2,3},{4,5},{6,7},{8,9},{10,11},{12,13},{14,15},{16,17},{18,... | collective-permute-start | bytes 402488 | tf_op jit(solution)/shard_map/ppermute | solution.py:22
  145.3 3.4 %collective-permute-start.23 = (f32[1,258,130]{2,1,0:T(8,128)S(1)}, f32[1,258,130]{2,1,0:T(8,128)S(1)}, u32[]{:S(2)}, u32[]{:S(2)}) collective-permute-start(f32[1,258,130]{2,1,0:T(8,128)S(1)} %get-tuple-element.26), channel_id=1, source_target_pairs={{1,0},{3,2},{5,4},{7,6},{9,8},{11,10},{13,12},{15,14},{17,16},{19,... | collective-permute-start | bytes 402488 | tf_op jit(solution)/shard_map/ppermute | solution.py:23
  171.3 2.2 %copy-start.2 = (f32[4,256,128]{2,1,0:T(8,128)S(1)}, f32[4,256,128]{2,1,0:T(8,128)}, u32[]{:S(2)}) copy-start(f32[4,256,128]{2,1,0:T(8,128)} %copy-done) | copy-start | bytes 1572868
  171.3 2.2 %copy-start.5 = (f32[4,256,128]{2,1,0:T(8,128)S(1)}, f32[4,256,128]{2,1,0:T(8,128)}, u32[]{:S(2)}) copy-start(f32[4,256,128]{2,1,0:T(8,128)} %copy-done.3) | copy-start | bytes 1572868
  171.4 2.2 %copy-start.17 = (f32[4,256,128]{2,1,0:T(8,128)S(1)}, f32[4,256,128]{2,1,0:T(8,128)}, u32[]{:S(2)}) copy-start(f32[4,256,128]{2,1,0:T(8,128)} %get-tuple-element.14) | copy-start | bytes 1572868
  (1 other events, 0.7 us)
